TPU v7x, 32 devices: a whole 2x2x4 slice. The times are simulated.
32 devices in a mesh: stn: 16 (over z, x, core), frq: 2 (over y).
Axes of the slice: x: 2, y: 2, z: 4, core: 2. Of those that a mesh axis runs over, the one named last changes fastest.
Arguments:
- spectra: bfloat16 [128, 2, 8192], P('stn', None, 'frq'), may hold values from -60 to 60, as said below
- pair_bin: int32 [4096, 1], P('stn'), may hold values from 0 to 15; in each aligned block of 256 rows (0 to 255, 256 to 511, ...) at most 34 rows name the same one
- pair_valid: int32 [4096], P('stn'), may hold values 0 or 1
- stack_in: float32 [16, 2048], P('stn', 'frq'), may hold values from -1.5 to 1.5
Outputs:
- stacks: float32 [16, 2048], P('stn', 'frq')
Inputs may be any that keep to these rules, and one draw needn't show every extreme that they name: `spectra`: values have rough magnitudes, differing from bin to bin. `pair_bin`: in the 256 rows of one index of stn no bin is named more than 34 times.
All inputs are finite; a program needn't handle non-finite values. No bound on the sum of `pair_valid` on one device may be relied on, other than what follows from the above.
Results may differ from a plain program's by a relative error of at most 0.008.
Values may be sent and summed in bfloat16 or wider, within the bound.
No kernel may reach another device: no remote copies, remote signals or barrier semaphores. Data moves between devices by JAX's collectives and lax.ppermute only.
A program may use at most 64 MiB of HBM per device.

v0:
```python
import math

import jax
import jax.numpy as jnp
from jax import lax
from jax.sharding import PartitionSpec as P

ROUNDS = 4
FREQ = 8192
SAMPLES = 32768
LAGS = 2048
WBLK = 32
LBLK = 512


def passed_along(value, axis, steps):
    count = lax.axis_size(axis)
    pairs = [(source, (source + steps) % count) for source in range(count)]
    return lax.ppermute(value, axis, pairs)


def whiten_band(spectra):
    count = spectra.shape[0]
    width = spectra.shape[2]
    values = spectra.astype(jnp.float32)
    blocks = values.reshape(count, 2, width // WBLK, WBLK)
    power = jnp.mean(blocks * blocks, axis=(1, 3), keepdims=True)
    return (blocks / jnp.sqrt(power + 1e-06)).reshape(count, 2, width).astype(jnp.bfloat16)


def cross_block(own, partner):
    own_f = own.astype(jnp.float32)
    part_f = partner.astype(jnp.float32)
    real_part = (
        own_f[:, 0][:, None, :] * part_f[:, 0][None] + own_f[:, 1][:, None, :] * part_f[:, 1][None]
    )
    imag_part = (
        own_f[:, 1][:, None, :] * part_f[:, 0][None] - own_f[:, 0][:, None, :] * part_f[:, 1][None]
    )
    joined = jnp.concatenate([real_part, imag_part], axis=2)
    return joined.reshape(own.shape[0] * partner.shape[0], -1).astype(jnp.bfloat16)


def lag_table(band_start, count, lag_start, lag_count):
    freq_index = band_start + 1 + lax.iota(jnp.int32, count)
    lag_index = lag_start - LAGS // 2 + lax.iota(jnp.int32, lag_count)
    product = freq_index[:, None] * lag_index[None, :] % SAMPLES
    angle = product.astype(jnp.float32) * (2.0 * math.pi / SAMPLES)
    return jnp.concatenate([jnp.cos(angle), -jnp.sin(angle)], axis=0).astype(jnp.bfloat16)


def local(spectra, pair_bin, pair_valid, stack_in):
    white = whiten_band(spectra)
    band_width = spectra.shape[2]
    band_start = lax.axis_index("frq") * band_width
    pieces = []
    for turn in range(ROUNDS):
        partner = passed_along(white, "stn", turn + 1)
        pieces.append(cross_block(white, partner))
    cross_all = jnp.concatenate(pieces, axis=0)
    lag_parts = []
    for block in range(LAGS // LBLK):
        table = lag_table(band_start, band_width, block * LBLK, LBLK)
        lag_parts.append(jnp.dot(cross_all, table, preferred_element_type=jnp.float32))
    partial_corr = jnp.concatenate(lag_parts, axis=1)
    valid = pair_valid.astype(jnp.float32)
    owners = lax.axis_size("stn")
    bins = pair_bin[:, 0]
    onehot = (bins[:, None] == lax.iota(jnp.int32, owners)[None, :]).astype(jnp.int32)
    onehot_float = onehot.astype(jnp.float32)
    mine = lax.psum_scatter(partial_corr, "frq", scatter_dimension=1, tiled=True)
    weighted = mine * (1.0 / FREQ) * valid[:, None]
    bin_sums = jnp.dot(
        onehot_float.T,
        weighted,
        precision=lax.Precision.HIGHEST,
        preferred_element_type=jnp.float32,
    )
    owned = lax.psum_scatter(bin_sums, "stn", scatter_dimension=0, tiled=True)
    return stack_in + owned


def solution(mesh):
    placed = (P("stn", None, "frq"), P("stn", None), P("stn"), P("stn", "frq"))
    return jax.shard_map(
        local, mesh=mesh, in_specs=placed, out_specs=P("stn", "frq"), check_vma=False
    )
```

profile of v0, /device:TPU:0, one launch (start us, length us, event | category | flops | bytes accessed | tf_op | source)
XLA Modules:
  0.0 315.9 jit_solution(10489845373939309425)
XLA Ops:
  6.5 0.0 reduce-scatter.2.cloned.1.call-start
  6.5 1.0 fusion.42
  7.5 0.2 reduce_sum.14
  7.7 0.2 reduce_sum.18
  7.9 0.2 div.21
  8.1 0.2 div.22
  8.4 1.0 fusion.51
  9.4 0.5 collective-permute-start
  9.9 2.5 collective-permute-start.1
  12.5 2.4 collective-permute-start.2
  14.9 1.6 collective-permute-start.3
  16.5 139.8 %cosine_convert_fusion.3 = (bf16[4096,512]{1,0:T(8,128)(2,1)}, bf16[4096,512]{1,0:T(8,128)(2,1)}, bf16[4096,512]{1,0:T(8,128)(2,1)S(1)}, bf16[4096,512]{1,0:T(8,...) fusion(s32[512]{0:T(512)S(1)} %iota_add_fusion.3, ...), kind=kLoop, calls=%fused_computation.55 | loop fusion | flops 142606336 | bytes 33576960 | tf_op jit(solution)/shard_map/convert.6
  156.3 0.0 collective-permute-done
  156.3 0.0 collective-permute-done.1
  156.4 0.0 collective-permute-done.2
  156.5 0.0 collective-permute-done.3
  156.5 2.3 fusion.33
  158.8 7.3 %fusion.12 = f32[256,512]{1,0:T(8,128)} fusion(bf16[4096,512]{1,0:T(8,128)(2,1)} %get-tuple-element.32, bf16[4096,512]{1,0:T(8,128)(2,1)} %get-tuple-element.31, bf16[64,4096]{1,0:T(8,128)(2,1)} %get-tuple-element.19, bf16[64,4096]{1,0:T(8,128)(2,1)} %get-tuple-element.20, bf16[64,4096]{1,0:T(8,128)(2,1)} %get-tuple-element.17, ...), kind=kOutput, calls=%fused_computation.30 | convolution fusion | flops 2197815296 | bytes 13107200 | tf_op jit(solution)/shard_map/dot_general | solution.py:64
  166.1 7.3 %fusion.16 = f32[256,512]{1,0:T(8,128)} fusion(bf16[4096,512]{1,0:T(8,128)(2,1)} %get-tuple-element.38, bf16[4096,512]{1,0:T(8,128)(2,1)} %get-tuple-element.39, bf16[64,4096]{1,0:T(8,128)(2,1)} %get-tuple-element.19, bf16[64,4096]{1,0:T(8,128)(2,1)} %get-tuple-element.20, bf16[64,4096]{1,0:T(8,128)(2,1)} %get-tuple-element.17, ...), kind=kOutput, calls=%fused_computation.34 | convolution fusion | flops 2197815296 | bytes 13107200 | tf_op jit(solution)/shard_map/dot_general | solution.py:64
  173.5 6.1 %fusion.20 = f32[256,512]{1,0:T(8,128)} fusion(bf16[4096,512]{1,0:T(8,128)(2,1)S(1)} %get-tuple-element.37, bf16[4096,512]{1,0:T(8,128)(2,1)} %get-tuple-element.40, bf16[64,4096]{1,0:T(8,128)(2,1)} %get-tuple-element.19, bf16[64,4096]{1,0:T(8,128)(2,1)} %get-tuple-element.20, bf16[64,4096]{1,0:T(8,128)(2,1)} %get-tuple-element.17, ...), kind=kOutput, calls=%fused_computation.38 | convolution fusion | flops 2197815296 | bytes 13107200 | tf_op jit(solution)/shard_map/dot_general | solution.py:64
  179.6 0.0 copy-start
  179.6 0.0 copy-start.1
  179.6 0.0 copy-start.2
  179.6 4.1 %fusion.24 = f32[256,512]{1,0:T(8,128)S(1)} fusion(bf16[4096,512]{1,0:T(8,128)(2,1)S(1)} %get-tuple-element.41, bf16[4096,512]{1,0:T(8,128)(2,1)S(1)} %get-tuple-element.42, bf16[64,4096]{1,0:T(8,128)(2,1)} %get-tuple-element.19, bf16[64,4096]{1,0:T(8,128)(2,1)} %get-tuple-element.20, bf16[64,4096]{1,0:T(8,128)(2,1)} %get-tuple-element.17, ...), kind=kOutput, calls=%fused_computation.42 | convolution fusion | flops 2197815296 | bytes 13107200 | tf_op jit(solution)/shard_map/dot_general | solution.py:64
  183.7 0.0 copy-done
  183.7 0.0 copy-done.1
  183.7 0.0 copy-done.2
  183.7 0.0 copy-start.4
  183.8 0.0 copy-start.5
  183.8 0.0 copy-start.6
  183.8 0.0 copy-start.3
  183.8 1.5 pad_maximum_fusion
  185.3 0.0 reduce-scatter.2.cloned.1.call-update
  185.3 0.0 all-reduce.3.cloned.1.call-start
  185.4 0.0 copy-done.4
  185.4 31.9 %reduce-scatter.2.cloned.1.call-done = f32[256,1024]{1,0:T(8,128)} async-done(((f32[256,2048]{1,0:T(8,128)}), f32[256,1024]{1,0:T(8,128)}) %reduce-scatter.2.cloned.1.call-update) | async-done | bytes 1048592 | tf_op jit(solution)/shard_map/reduce_scatter | solution.py:71
  217.4 0.0 copy-done.5
  217.4 2.6 fusion.31
  219.9 0.0 all-reduce.3.cloned.1.call-update
  220.0 0.0 copy-done.6
  220.0 0.6 dynamic-slice
  220.6 86.4 %all-reduce.3.cloned.1.call-done = f32[16,1024]{1,0:T(8,128)} async-done(((f32[16,1024]{1,0:T(8,128)}), f32[16,1024]{1,0:T(8,128)}) %all-reduce.3.cloned.1.call-update) | async-done | bytes 65552
  307.0 0.0 copy-done.3
  307.0 2.0 dynamic-slice_add_fusion
  (14 shorter events, 0.2 us)
Async XLA Ops:
  6.5 210.8 %reduce-scatter.2.cloned.1.call-start = ((), (), s32[]{:S(2)}) async-start(), calls=%async_computation.1 | async-start | bytes 3145728 | tf_op jit(solution)/shard_map/reduce_scatter | solution.py:71
  9.4 146.9 %collective-permute-start = (bf16[8,2,4096]{2,0,1:T(8,128)(2,1)S(1)}, bf16[8,2,4096]{2,0,1:T(8,128)(2,1)S(1)}, u32[]{:S(2)}, u32[]{:S(2)}) collective-permute-start(bf16[8,2,4096]{2,0,1:T(8,128)(2,1)S(1)} %get-tuple-element.6), channel_id=1, source_target_pairs={{0,2},{2,4},{4,6},{6,8},{8,10},{10,12},{12,14},{14,16},{16,18},{18... | collective-permute-start | bytes 393224 | tf_op jit(solution)/shard_map/ppermute | solution.py:19
  9.9 146.4 %collective-permute-start.1 = (bf16[8,2,4096]{2,0,1:T(8,128)(2,1)S(1)}, bf16[8,2,4096]{2,0,1:T(8,128)(2,1)S(1)}, u32[]{:S(2)}, u32[]{:S(2)}) collective-permute-start(bf16[8,2,4096]{2,0,1:T(8,128)(2,1)S(1)} %get-tuple-element.6), channel_id=1, source_target_pairs={{0,4},{2,6},{4,8},{6,10},{8,12},{10,14},{12,16},{14,18},{16,20},{1... | collective-permute-start | bytes 393224 | tf_op jit(solution)/shard_map/ppermute | solution.py:19
  12.5 144.0 %collective-permute-start.2 = (bf16[8,2,4096]{2,0,1:T(8,128)(2,1)S(1)}, bf16[8,2,4096]{2,0,1:T(8,128)(2,1)S(1)}, u32[]{:S(2)}, u32[]{:S(2)}) collective-permute-start(bf16[8,2,4096]{2,0,1:T(8,128)(2,1)S(1)} %get-tuple-element.6), channel_id=1, source_target_pairs={{0,6},{2,8},{4,10},{6,12},{8,14},{10,16},{12,18},{14,20},{16,22},{... | collective-permute-start | bytes 393224 | tf_op jit(solution)/shard_map/ppermute | solution.py:19
  14.9 141.6 %collective-permute-start.3 = (bf16[8,2,4096]{2,0,1:T(8,128)(2,1)S(1)}, bf16[8,2,4096]{2,0,1:T(8,128)(2,1)S(1)}, u32[]{:S(2)}, u32[]{:S(2)}) collective-permute-start(bf16[8,2,4096]{2,0,1:T(8,128)(2,1)S(1)} %get-tuple-element.6), channel_id=1, source_target_pairs={{0,8},{2,10},{4,12},{6,14},{8,16},{10,18},{12,20},{14,22},{16,24},... | collective-permute-start | bytes 393224 | tf_op jit(solution)/shard_map/ppermute | solution.py:19
  179.6 4.1 %copy-start = (f32[256,512]{1,0:T(8,128)S(1)}, f32[256,512]{1,0:T(8,128)}, u32[]{:S(2)}) copy-start(f32[256,512]{1,0:T(8,128)} %fusion.12) | copy-start | bytes 1572868
  179.6 4.1 %copy-start.1 = (f32[256,512]{1,0:T(8,128)S(1)}, f32[256,512]{1,0:T(8,128)}, u32[]{:S(2)}) copy-start(f32[256,512]{1,0:T(8,128)} %fusion.16) | copy-start | bytes 1572868
  179.6 4.1 %copy-start.2 = (f32[256,512]{1,0:T(8,128)S(1)}, f32[256,512]{1,0:T(8,128)}, u32[]{:S(2)}) copy-start(f32[256,512]{1,0:T(8,128)} %fusion.20) | copy-start | bytes 1572868
  183.7 1.6 copy-start.4
  183.8 33.6 %copy-start.5 = (s32[256,1]{0,1:T(1,128)S(1)}, s32[256,1]{0,1:T(1,128)}, u32[]{:S(2)}) copy-start(s32[256,1]{0,1:T(1,128)} %param.5) | copy-start | bytes 3076
  183.8 36.2 %copy-start.6 = (u32[32]{0:T(128)S(1)}, u32[32]{0:T(128)}, u32[]{:S(2)}) copy-start(u32[32]{0:T(128)} %constant.59) | copy-start | bytes 388
  183.8 123.3 %copy-start.3 = (f32[1,1024]{1,0:T(1,128)S(1)}, f32[1,1024]{1,0:T(1,128)}, u32[]{:S(2)}) copy-start(f32[1,1024]{1,0:T(1,128)} %param.7) | copy-start | bytes 12292
  185.3 121.7 %all-reduce.3.cloned.1.call-start = ((), (), s32[]{:S(2)}) async-start(), calls=%async_computation.2 | async-start | bytes 131072
Sparse Core Ops, SparseCore 0:
  185.5 31.8 reduce-scatter.1
  220.8 86.1 all-reduce.2
where the time goes:
time: 317 us; the launch traced here: 316 us
  other arithmetic  148 us (47%)
  waiting for transfers between devices  118 us (37%)
  matrix products  27.5 us (9%)
  between operations  13.6 us (4%)
  starting transfers between devices  7.12 us (2%)
    another operation x1, other arithmetic  140 us
    unnamed x3, waiting for transfers between devices  86.5 us
    reduce_scatter x1, waiting for transfers between devices, local(): lax.psum_scatter(partial_corr, 'frq', scatter_dimension=1, tiled=True)  31.9 us
    dot_general x4, matrix products, local(): jnp.dot(cross_all, table, preferred_element_type=jnp.float32)  24.9 us
    ppermute x4, starting transfers between devices, passed_along(): return lax.ppermute(value, axis, pairs)  7.07 us
  transfers between devices with their start and end apart: 6, of which 2 were waited for; matrix products, arithmetic and copies ran while one was open for 44% of the time, Pallas kernels for 0%

commit v1 on v0

v1 whole, which is shorter than its diff:
```python
import functools
import math

import jax
import jax.numpy as jnp
from jax import lax
from jax.experimental import pallas as pl
from jax.experimental.pallas import tpu as pltpu
from jax.sharding import PartitionSpec as P

ROUNDS = 4
SAMPLES = 32768
WBLK = 32
LANES = 128


def whiten_band(spectra):
    count, _, width = spectra.shape
    values = spectra.astype(jnp.float32)
    blocks = values.reshape(count, 2, width // WBLK, WBLK)
    power = jnp.mean(blocks * blocks, axis=(1, 3), keepdims=True)
    return (blocks / jnp.sqrt(power + 1e-06)).reshape(count, 2, width).astype(jnp.bfloat16)


def code_rows(pair_bin, pair_valid, own, owners, block):
    codes = jnp.where(pair_valid != 0, pair_bin[:, 0] + 1, 0).astype(jnp.float32)
    rows = codes.reshape(ROUNDS, block, block).transpose(1, 0, 2)
    place = lax.iota(jnp.int32, owners)[None, :]
    source = (own - 1 - lax.iota(jnp.int32, ROUNDS)[:, None]) % owners
    chosen = (place == source).astype(jnp.float32)
    return jnp.einsum("irj,rd->idj", rows, chosen, precision=lax.Precision.HIGHEST).reshape(
        block, owners * block
    )


def bin_kernel(owners, copies, block, halves, got_ref, sums_ref):
    stations = owners * block
    lanes = got_ref.shape[2]
    tile = lambda place: got_ref[:, place * block : (place + 1) * block, :].reshape(stations, lanes)
    pieces = [tile(place) for place in range(2 * halves)]
    codes = [tile(2 * halves + place) for place in range(stations // lanes)]
    codes = jnp.concatenate(codes, axis=1).astype(jnp.float32)
    right = jnp.concatenate(pieces, axis=1)
    left = [piece.astype(jnp.float32) for piece in pieces]
    for owner in range(owners):
        chosen = jnp.where(codes == float(owner + 1), 1.0, 0.0).astype(jnp.bfloat16)
        mixed = jnp.dot(chosen, right, preferred_element_type=jnp.float32)
        for half in range(halves):
            own_re, own_im = left[2 * half], left[2 * half + 1]
            mix_re = mixed[:, 2 * half * lanes : (2 * half + 1) * lanes]
            mix_im = mixed[:, (2 * half + 1) * lanes : (2 * half + 2) * lanes]
            real = jnp.sum(own_re * mix_re + own_im * mix_im, axis=0, keepdims=True)
            imag = jnp.sum(own_im * mix_re - own_re * mix_im, axis=0, keepdims=True)
            for copy in range(copies):
                place = owner * copies + copy
                sums_ref[place, half : half + 1, :] = real
                sums_ref[place, halves + half : halves + half + 1, :] = imag


def turn(product, period):
    angle = lax.rem(product, jnp.int32(period)).astype(jnp.float32) * (2.0 * math.pi / period)
    return jnp.cos(angle), jnp.sin(angle)


def iota(shape, dimension):
    return lax.broadcasted_iota(jnp.int32, shape, dimension)


def lag_kernel(owners, bands, halves, scale, band_ref, sums_ref, stack_ref, out_ref):
    sources = owners * bands
    fine = halves * sums_ref.shape[2]
    coarse = SAMPLES // fine
    turns = out_ref.shape[1] // coarse
    exact = lax.Precision.HIGHEST
    part = lambda row: sums_ref[:, row, :]
    real = jnp.concatenate([part(half) for half in range(halves)], axis=1)
    imag = jnp.concatenate([part(halves + half) for half in range(halves)], axis=1)
    shape = (coarse, sources)
    source = iota(shape, 1)
    upper = lax.rem(source, jnp.int32(bands)) * owners + lax.div(source, jnp.int32(bands))
    cos1, sin1 = turn(upper * iota(shape, 0), coarse)
    first = jnp.concatenate(
        [jnp.concatenate([cos1, -sin1], axis=1), jnp.concatenate([sin1, cos1], axis=1)], axis=0
    )
    mixed = jnp.dot(
        first, jnp.concatenate([real, imag], axis=0), precision=exact, preferred_element_type=jnp.float32
    )
    shape = (coarse, fine)
    cos2, sin2 = turn((iota(shape, 1) + 1) * iota(shape, 0), SAMPLES)
    mix_re, mix_im = mixed[:coarse], mixed[coarse:]
    turned = jnp.concatenate([mix_re * cos2 - mix_im * sin2, mix_re * sin2 + mix_im * cos2], axis=1)
    shape = (turns, fine)
    step = iota(shape, 0) + band_ref[0] * turns + (SAMPLES - bands * turns // 2)
    cos3, sin3 = turn((iota(shape, 1) + 1) * step, fine)
    last = jnp.concatenate([cos3, -sin3], axis=1)
    lags = lax.dot_general(
        last, turned, (((1,), (1,)), ((), ())), precision=exact, preferred_element_type=jnp.float32
    )
    for row in range(turns):
        place = slice(row * coarse, (row + 1) * coarse)
        out_ref[:, place] = stack_ref[:, place] + lags[row : row + 1, :] * scale


def whole(memory=pltpu.VMEM):
    return pl.BlockSpec(memory_space=memory)


def local(spectra, pair_bin, pair_valid, stack_in):
    block, _, width = spectra.shape
    owners, bands = lax.axis_size("stn"), lax.axis_size("frq")
    own, band = lax.axis_index("stn"), lax.axis_index("frq")
    fine = width // owners
    lanes = min(fine, LANES)
    halves = fine // lanes
    white = whiten_band(spectra)
    tiles = white.reshape(block, 2, owners, halves, lanes).transpose(2, 3, 1, 0, 4)
    tiles = tiles.reshape(owners, halves * 2 * block, lanes)
    codes = code_rows(pair_bin, pair_valid, own, owners, block).astype(jnp.bfloat16)
    codes = codes.reshape(block, -1, lanes).transpose(1, 0, 2).reshape(-1, lanes)
    codes = jnp.broadcast_to(codes[None], (owners,) + codes.shape)
    got = lax.all_to_all(jnp.concatenate([tiles, codes], axis=1), "stn", 0, 0, tiled=True)
    sums = pl.pallas_call(
        functools.partial(bin_kernel, owners, bands, block, halves),
        out_shape=jax.ShapeDtypeStruct((owners * bands, 2 * halves, lanes), jnp.float32),
        in_specs=[whole()],
        out_specs=whole(),
    )(got)
    sums = lax.all_to_all(sums, ("stn", "frq"), 0, 0, tiled=True)
    return pl.pallas_call(
        functools.partial(lag_kernel, owners, bands, halves, 1.0 / (width * bands)),
        out_shape=jax.ShapeDtypeStruct(stack_in.shape, jnp.float32),
        in_specs=[whole(pltpu.SMEM), whole(), whole()],
        out_specs=whole(),
    )(band[None], sums, stack_in)


def solution(mesh):
    placed = (P("stn", None, "frq"), P("stn", None), P("stn"), P("stn", "frq"))
    return jax.shard_map(
        local, mesh=mesh, in_specs=placed, out_specs=P("stn", "frq"), check_vma=False
    )
```

time: 317 us -> 35.9 us (0.11)
  other arithmetic: 148 us -> 2.13 us
  waiting for transfers between devices: 118 us -> 7.6 us
  matrix products: 27.5 us -> 0.23 us
  blocking collectives: 0 us -> 15.7 us
  between operations: 13.6 us -> 0.1 us
  Pallas kernels: 0 us -> 5.58 us
  starting transfers between devices: 7.12 us -> 2.54 us
    another operation x1 -> x0, other arithmetic: 140 us -> none
    unnamed x3 -> x0, waiting for transfers between devices: 86.5 us -> none
    reduce_scatter x1 -> x0, waiting for transfers between devices: 31.9 us -> none  [local(): lax.psum_scatter(partial_corr, 'frq', scatter_dimension=1, tiled=True)]
    dot_general x5 -> x1, matrix products: 27.5 us -> 0.23 us  [code_rows(): jnp.einsum('irj,rd->idj', rows, chosen, precision=lax.Precision.HIGHEST)]
    all_to_all x0 -> x1, blocking collectives: none -> 15.7 us  [local(): lax.all_to_all(jnp.concatenate([tiles, codes], axis=1), 'stn', 0, 0, tile...]
    all_to_all x0 -> x1, waiting for transfers between devices: none -> 7.6 us  [local(): sums = lax.all_to_all(sums, ('stn', 'frq'), 0, 0, tiled=True)]
    ppermute x4 -> x0, starting transfers between devices: 7.07 us -> none  [passed_along(): return lax.ppermute(value, axis, pairs)]
    pallas_call x0 -> x2, Pallas kernels: none -> 5.58 us  [the longest x1 3.2 us: local(): pl.pallas_call(functools.partial(lag_kernel, owners, bands, halves, 1.0 /...]
  transfers between devices with their start and end apart: 6 -> 1, of which waited for: 2 -> 1; matrix products, arithmetic and copies ran while one was open for 44% -> 0% of each run, Pallas kernels for 0% -> 0%
where the time goes in v1:
time: 35.9 us; the launch traced here: 35.6 us
  blocking collectives  15.7 us (44%)
  waiting for transfers between devices  7.6 us (21%)
  Pallas kernels  5.58 us (16%)
  starting transfers between devices  2.54 us (7%)
  other arithmetic  2.13 us (6%)
  local copies, waits for them, and re-layouts  1.71 us (5%)
    all_to_all x1, blocking collectives, local(): lax.all_to_all(jnp.concatenate([tiles, codes], axis=1), 'stn', 0, 0, tile...  15.7 us
    all_to_all x1, waiting for transfers between devices, local(): sums = lax.all_to_all(sums, ('stn', 'frq'), 0, 0, tiled=True)  7.6 us
    pallas_call x1, Pallas kernels, local(): pl.pallas_call(functools.partial(lag_kernel, owners, bands, halves, 1.0 /...  3.2 us
    all_to_all x1, starting transfers between devices, local(): sums = lax.all_to_all(sums, ('stn', 'frq'), 0, 0, tiled=True)  2.54 us
    pallas_call x1, Pallas kernels, local(): pl.pallas_call(functools.partial(bin_kernel, owners, bands, block, halves...  2.38 us
  transfers between devices with their start and end apart: 1, of which 1 were waited for; matrix products, arithmetic and copies ran while one was open for 0% of the time, Pallas kernels for 0%

profile of v1, /device:TPU:0, one launch (start us, length us, event | category | flops | bytes accessed | tf_op | source)
XLA Modules:
  0.0 35.6 jit_solution(11255174737482427734)
XLA Ops:
  0.0 0.0 copy-start
  0.0 0.7 %broadcast_add_fusion = s32[256,1]{0,1:T(1,128)S(1)} fusion(s32[256,1]{0,1:T(1,128)} %param.5), kind=kLoop, calls=%fused_computation.18 | loop fusion | flops 256 | bytes 2048 | tf_op jit(solution)/shard_map/add | solution.py:26
  0.7 0.7 %fusion.6 = f32[256]{0:T(256)S(1)} fusion(s32[256]{0:T(256)S(1)} %bitcast.14, s32[256]{0:T(256)} %param.6), kind=kLoop, calls=%fused_computation.15 | loop fusion | flops 768 | bytes 3072 | tf_op jit(solution)/shard_map/convert_element_type | solution.py:26
  1.4 0.1 reshape.54
  1.5 0.2 fusion
  1.7 0.1 copy.8
  1.8 0.1 convert_element_type.28
  1.9 0.0 copy-done
  1.9 0.3 fusion.1
  2.3 0.2 reduce_sum.14
  2.5 0.2 reduce_sum.18
  2.7 0.2 div.21
  2.9 0.2 div.22
  3.1 0.1 fusion.2
  3.3 0.1 reshape.52
  3.4 0.1 copy.6
  3.5 15.7 %all_to_all.10.got_ref = bf16[16,40,128]{2,1,0:T(8,128)(2,1)} all-to-all(bf16[16,40,128]{2,1,0:T(8,128)(2,1)S(1)} %pad_maximum_fusion), channel_id=1, replica_groups=mesh['stn'=16,'frq'=2] {'stn'}, dimensions={0} | all-to-all | bytes 327680 | tf_op jit(solution)/shard_map/all_to_all | solution.py:121
  19.3 2.4 %shard_map.46 = f32[32,4,128]{2,1,0:T(4,128)} custom-call(bf16[16,40,128]{2,1,0:T(8,128)(2,1)} %all_to_all.10.got_ref), custom_call_target="tpu_custom_call" | custom-call | tf_op jit(solution)/shard_map/pallas_call | solution.py:122
  21.6 2.5 %all-to-all-start.1 = ((f32[32,4,128]{2,1,0:T(4,128)}), f32[32,4,128]{2,1,0:T(4,128)S(1)}, u32[]{:S(2)}, u32[]{:S(2)}) async-start(f32[32,4,128]{2,1,0:T(4,128)} %shard_map.46), calls=%async_computation.1 | async-start | bytes 131072 | tf_op jit(solution)/shard_map/all_to_all | solution.py:128
  24.2 7.6 %all-to-all-done.1.sums_ref = f32[32,4,128]{2,1,0:T(4,128)S(1)} async-done(((f32[32,4,128]{2,1,0:T(4,128)}), f32[32,4,128]{2,1,0:T(4,128)S(1)}, u32[]{:S(2)}, u32[]{:S(2)}) %all-to-all-start.1) | async-done | bytes 65568 | tf_op jit(solution)/shard_map/all_to_all | solution.py:128
  31.8 0.0 copy-start.1
  31.8 0.6 %copy-done.1 = f32[32,4,128]{2,1,0:T(4,128)} copy-done((f32[32,4,128]{2,1,0:T(4,128)}, f32[32,4,128]{2,1,0:T(4,128)S(1)}, u32[]{:S(2)}) %copy-start.1) | copy-done | bytes 65560
  32.4 3.2 %shard_map.47 = f32[1,1024]{1,0:T(1,128)} custom-call(s32[1]{0:T(128)} %bitcast.3.band_ref, f32[32,4,128]{2,1,0:T(4,128)} %copy-done.1, f32[1,1024]{1,0:T(1,128)} %stack_ref.1), custom_call_target="tpu_custom_call" | custom-call | tf_op jit(solution)/shard_map/pallas_call | solution.py:129
  (4 shorter events, 0.0 us)
Async XLA Ops:
  0.0 1.9 %copy-start = (bf16[8,2,4096]{2,1,0:T(2,128)(2,1)S(1)}, bf16[8,2,4096]{2,1,0:T(2,128)(2,1)}, u32[]{:S(2)}) copy-start(bf16[8,2,4096]{2,1,0:T(2,128)(2,1)} %param.4) | copy-start | bytes 393220
  21.6 10.2 %all-to-all-start.1 = ((f32[32,4,128]{2,1,0:T(4,128)}), f32[32,4,128]{2,1,0:T(4,128)S(1)}, u32[]{:S(2)}, u32[]{:S(2)}) async-start(f32[32,4,128]{2,1,0:T(4,128)} %shard_map.46), calls=%async_computation.1 | async-start | bytes 131072 | tf_op jit(solution)/shard_map/all_to_all | solution.py:128
  31.8 0.6 %copy-start.1 = (f32[32,4,128]{2,1,0:T(4,128)}, f32[32,4,128]{2,1,0:T(4,128)S(1)}, u32[]{:S(2)}) copy-start(f32[32,4,128]{2,1,0:T(4,128)S(1)} %all-to-all-done.1.sums_ref) | copy-start | bytes 196612

commit v2 on v1

v2 whole, which is shorter than its diff:
```python
import functools
import math

import jax
import jax.numpy as jnp
from jax import lax
from jax.experimental import pallas as pl
from jax.experimental.pallas import tpu as pltpu
from jax.sharding import PartitionSpec as P

ROUNDS = 4
SAMPLES = 32768
WBLK = 32
LANES = 128
TILE = 8


def iota(shape, dimension):
    return lax.broadcasted_iota(jnp.int32, shape, dimension)


def split(value):
    upper = value.astype(jnp.bfloat16)
    return upper, (value - upper.astype(jnp.float32)).astype(jnp.bfloat16)


def dot(left, right):
    return jnp.dot(left, right, preferred_element_type=jnp.float32)


def pack_kernel(owners, bands, block, scale, spectra_ref, bin_ref, valid_ref, stack_ref, *refs):
    pack_ref, held_ref, *tables, bins, valids, sems = refs
    stations = owners * block
    pairs = bins.shape[1]
    lanes = pack_ref.shape[3]
    copies = [
        pltpu.make_async_copy(bin_ref, bins, sems.at[0]),
        pltpu.make_async_copy(valid_ref, valids, sems.at[1]),
        pltpu.make_async_copy(stack_ref, held_ref, sems.at[2]),
    ]
    tiles = pack_ref.shape[1] - stations // lanes * (block // 2)
    if len(spectra_ref.shape) == 3:
        halves = tiles // block
        for place in range(owners * halves):
            source = spectra_ref.at[:, :, pl.ds(place * lanes, lanes)]
            target = pack_ref.at[place // halves, pl.ds(place % halves * block, block)]
            copies.append(pltpu.make_async_copy(source, target, sems.at[3 + place]))
    else:
        target = pack_ref.at[:, pl.ds(0, tiles)]
        copies.append(pltpu.make_async_copy(spectra_ref, target, sems.at[3]))
    for copy in copies:
        copy.start()
    place = iota((block, pairs), 1)
    mine = lax.rem(lax.div(place, block), block) == iota((block, pairs), 0)
    place = iota((pairs, stations), 0)
    ahead = lax.axis_index("stn") + (owners - 1)
    other = lax.rem(ahead - lax.div(place, block * block), owners) * block + lax.rem(place, block)
    right = jnp.where(other == iota((pairs, stations), 1), 1.0, 0.0).astype(jnp.bfloat16)
    fill_tables(owners, bands, scale, *tables)
    copies[0].wait()
    copies[1].wait()
    codes = jnp.where(valids[...] != 0, bins[...] + 1, 0).astype(jnp.float32)
    left = jnp.where(mine, jnp.broadcast_to(codes, (block, pairs)), 0.0).astype(jnp.bfloat16)
    codes = dot(left, right)
    for place in range(stations // lanes):
        piece = codes[:, place * lanes : (place + 1) * lanes].reshape(block // 2, 2, lanes)
        piece = piece.astype(jnp.bfloat16)
        start = tiles + place * (block // 2)
        for owner in range(owners):
            pack_ref[owner, start : start + block // 2] = piece
    for copy in copies[2:]:
        copy.wait()


def bin_kernel(owners, copies, block, halves, got_ref, sums_ref, rows_ref):
    stations = owners * block
    lanes = got_ref.shape[2]
    start = 2 * halves * block
    codes = [
        got_ref[:, start + place * block : start + (place + 1) * block, :].reshape(stations, lanes)
        for place in range(stations // lanes)
    ]
    codes = jnp.concatenate(codes, axis=1).astype(jnp.float32)
    shape = (lanes, lanes)
    same = lax.div(iota(shape, 0), WBLK) == lax.div(iota(shape, 1), WBLK)
    same = jnp.where(same, 0.5 / WBLK, 0.0).astype(jnp.bfloat16)
    pieces = []
    for half in range(halves):
        raw = got_ref[:, 2 * half * block : 2 * (half + 1) * block, :].astype(jnp.float32)
        rows_ref[half] = raw.reshape(2 * stations, lanes)
        raw = [rows_ref[half, pl.ds(part, stations, stride=2), :] for part in range(2)]
        upper, lower = split(raw[0] * raw[0] + raw[1] * raw[1])
        scale = lax.rsqrt(dot(upper, same) + dot(lower, same) + 1e-06)
        pieces += [(value * scale).astype(jnp.bfloat16) for value in raw]
    right = jnp.concatenate(pieces, axis=1)
    left = [piece.astype(jnp.float32) for piece in pieces]
    for owner in range(owners):
        chosen = jnp.where(codes == float(owner + 1), 1.0, 0.0).astype(jnp.bfloat16)
        mixed = dot(chosen, right)
        for half in range(halves):
            own_re, own_im = left[2 * half], left[2 * half + 1]
            mix_re = mixed[:, 2 * half * lanes : (2 * half + 1) * lanes]
            mix_im = mixed[:, (2 * half + 1) * lanes : (2 * half + 2) * lanes]
            real = jnp.sum(own_re * mix_re + own_im * mix_im, axis=0, keepdims=True)
            imag = jnp.sum(own_im * mix_re - own_re * mix_im, axis=0, keepdims=True)
            for copy in range(copies):
                place = owner * copies + copy
                sums_ref[place, half : half + 1, :] = real
                sums_ref[place, halves + half : halves + half + 1, :] = imag


def turn(product, period, ahead=0.0):
    angle = lax.rem(product, jnp.int32(period)).astype(jnp.float32) * (2.0 * math.pi / period) + ahead
    return jnp.cos(angle), jnp.sin(angle)


def powers(factor, period, count, store, ahead=0.0):
    width = factor.shape[1]
    near_cos, near_sin = turn(factor * iota((TILE, width), 0), period, ahead)
    far_cos, far_sin = turn(factor * (TILE * iota((count // TILE, width), 0)), period)
    for step in range(count // TILE):
        cos, sin = far_cos[step : step + 1, :], far_sin[step : step + 1, :]
        store(step * TILE, near_cos * cos - near_sin * sin, near_sin * cos + near_cos * sin)


def fill_tables(owners, bands, scale, first_ref, turn_ref, last_ref):
    coarse, span = first_ref.shape[0] // 2, first_ref.shape[1] // 3
    turns, fine = last_ref.shape[0] // 2, last_ref.shape[1] // 2

    width = max(span, LANES)
    column = lax.rem(iota((1, width), 1), span)
    source = lax.rem(column, owners * bands)
    factor = lax.rem(source, bands) * owners + lax.div(source, bands)
    ahead = jnp.where(column < owners * bands, 0.0, 0.5 * math.pi)

    def store_first(start, cos, sin):
        for begin, value in ((start, cos), (coarse + start, sin)):
            upper, lower = split(value)
            for place in range(0, 2 * span, width):
                first_ref[begin : begin + TILE, place : place + width] = upper
            first_ref[begin : begin + TILE, 2 * span :] = lower[:, :span]

    def store_turn(start, cos, sin):
        turn_ref[start : start + TILE, :] = cos
        turn_ref[coarse + start : coarse + start + TILE, :] = sin

    powers(factor, coarse, coarse, store_first, ahead)
    powers(iota((1, fine), 1) + 1, SAMPLES, coarse, store_turn)
    shape = (turns, fine)
    band = lax.axis_index("frq")
    step = iota(shape, 0) + band * turns + (SAMPLES - bands * turns // 2)
    cos, sin = turn((iota(shape, 1) + 1) * step, fine)
    upper, lower = split(jnp.concatenate([cos, -sin], axis=1) * scale)
    last_ref[...] = jnp.concatenate([upper, lower], axis=0)


def lag_kernel(halves, first_ref, turn_ref, last_ref, sums_ref, stack_ref, out_ref):
    coarse = first_ref.shape[0] // 2
    turns = last_ref.shape[0] // 2
    part = lambda row: sums_ref[:, row, :]
    real = jnp.concatenate([part(half) for half in range(halves)], axis=1)
    imag = jnp.concatenate([part(halves + half) for half in range(halves)], axis=1)
    upper, lower = split(jnp.concatenate([real, imag], axis=0))
    mixed = dot(first_ref[...], jnp.concatenate([upper, lower, upper], axis=0))
    mix_re, mix_im = mixed[:coarse], mixed[coarse:]
    cos, sin = turn_ref[:coarse, :], turn_ref[coarse:, :]
    turned = jnp.concatenate([mix_re * cos - mix_im * sin, mix_re * sin + mix_im * cos], axis=1)
    upper, lower = split(turned)
    across = lambda left, right: lax.dot_general(
        left, right, (((1,), (1,)), ((), ())), preferred_element_type=jnp.float32
    )
    lags = across(last_ref[...], upper)
    lags = lags[:turns] + lags[turns:] + across(last_ref[:turns, :], lower)
    for row in range(turns):
        place = slice(row * coarse, (row + 1) * coarse)
        out_ref[:, place] = stack_ref[:, place] + lags[row : row + 1, :]


def whole(memory=pltpu.VMEM):
    return pl.BlockSpec(memory_space=memory)


def near(value):
    return pltpu.with_memory_space_constraint(value, pltpu.VMEM)


def local(spectra, pair_bin, pair_valid, stack_in):
    block, _, width = spectra.shape
    owners, bands = lax.axis_size("stn"), lax.axis_size("frq")
    stations = owners * block
    pairs = pair_valid.shape[0]
    fine = width // owners
    lanes = min(fine, LANES)
    halves = fine // lanes
    coarse = SAMPLES // fine
    turns = stack_in.shape[1] // coarse
    if lanes < LANES:
        spectra = spectra.reshape(block, 2, owners, halves, lanes).transpose(2, 3, 0, 1, 4)
        spectra = spectra.reshape(owners, halves * block, 2, lanes)
    rows = halves * block + stations // lanes * (block // 2)
    packed, stack, *tables = pl.pallas_call(
        functools.partial(pack_kernel, owners, bands, block, 1.0 / (width * bands)),
        out_shape=[
            pltpu.VMEM((owners, rows, 2, lanes), jnp.bfloat16),
            pltpu.VMEM(stack_in.shape, jnp.float32),
            pltpu.VMEM((2 * coarse, 6 * owners * bands), jnp.bfloat16),
            pltpu.VMEM((2 * coarse, fine), jnp.float32),
            pltpu.VMEM((2 * turns, 2 * fine), jnp.bfloat16),
        ],
        in_specs=[whole(pl.ANY)] * 4,
        out_specs=[whole()] * 5,
        scratch_shapes=[
            pltpu.VMEM((1, pairs), jnp.int32),
            pltpu.VMEM((1, pairs), jnp.int32),
            pltpu.SemaphoreType.DMA((3 + owners * halves,)),
        ],
    )(spectra, pair_bin.reshape(1, pairs), pair_valid.reshape(1, pairs), stack_in)
    got = lax.all_to_all(packed.reshape(owners, 2 * rows, lanes), "stn", 0, 0, tiled=True)
    sums = pl.pallas_call(
        functools.partial(bin_kernel, owners, bands, block, halves),
        out_shape=pltpu.VMEM((owners * bands, 2 * halves, lanes), jnp.float32),
        in_specs=[whole()],
        out_specs=whole(),
        scratch_shapes=[pltpu.VMEM((halves, 2 * stations, lanes), jnp.float32)],
    )(near(got))
    sums = lax.all_to_all(sums, ("stn", "frq"), 0, 0, tiled=True)
    return pl.pallas_call(
        functools.partial(lag_kernel, halves),
        out_shape=jax.ShapeDtypeStruct(stack_in.shape, jnp.float32),
        in_specs=[whole()] * 5,
        out_specs=whole(),
    )(*[near(value) for value in (*tables, sums, stack)])


def solution(mesh):
    placed = (P("stn", None, "frq"), P("stn", None), P("stn"), P("stn", "frq"))
    return jax.shard_map(
        local, mesh=mesh, in_specs=placed, out_specs=P("stn", "frq"), check_vma=False
    )
```

time: 35.9 us -> 28.9 us (0.81)
  blocking collectives: 15.7 us -> 25.4 us
  waiting for transfers between devices: 7.6 us -> 0 us
  starting transfers between devices: 2.54 us -> 0 us
  Pallas kernels: 5.58 us -> 3.28 us
  other arithmetic: 2.13 us -> 0 us
  local copies, waits for them, and re-layouts: 1.71 us -> 0 us
    all_to_all x1 -> x2, blocking collectives: 15.7 us -> 25.4 us  [the longest x1 15.6 us: local(): lax.all_to_all(packed.reshape(owners, 2 * rows, lanes), 'stn', 0, 0, tile...]
    all_to_all x1 -> x0, waiting for transfers between devices: 7.6 us -> none  [local(): sums = lax.all_to_all(sums, ('stn', 'frq'), 0, 0, tiled=True)]
    all_to_all x1 -> x0, starting transfers between devices: 2.54 us -> none  [local(): sums = lax.all_to_all(sums, ('stn', 'frq'), 0, 0, tiled=True)]
    pallas_call x1, Pallas kernels: 2.38 us -> 1.02 us  [local(): pl.pallas_call(functools.partial(bin_kernel, owners, bands, block, halves...]
    pallas_call x1 -> x2, Pallas kernels: 3.2 us -> 2.27 us  [the longest x1 1.24 us: local(): pl.pallas_call(functools.partial(pack_kernel, owners, bands, block, 1.0 /...]
    convert_element_type x2 -> x0, other arithmetic: 0.83 us -> none  [the longest x1 0.68 us: code_rows(): jnp.where(pair_valid != 0, pair_bin[:, 0] + 1, 0).astype(jnp.float32)]
    add x1 -> x0, other arithmetic: 0.72 us -> none  [code_rows(): pair_bin[:, 0] + 1]
    unnamed x4 -> x0, local copies, waits for them, and re-layouts: 0.62 us -> none
  transfers between devices with their start and end apart: 1 -> 0, of which waited for: 1 -> 0; matrix products, arithmetic and copies ran while one was open for 0% -> 0% of each run, Pallas kernels for 0% -> 0%
where the time goes in v2:
time: 28.9 us; the launch traced here: 28.7 us
  blocking collectives  25.4 us (88%)
  Pallas kernels  3.28 us (11%)
    all_to_all x1, blocking collectives, local(): lax.all_to_all(packed.reshape(owners, 2 * rows, lanes), 'stn', 0, 0, tile...  15.6 us
    all_to_all x1, blocking collectives, local(): sums = lax.all_to_all(sums, ('stn', 'frq'), 0, 0, tiled=True)  9.8 us
    pallas_call x1, Pallas kernels, local(): pl.pallas_call(functools.partial(pack_kernel, owners, bands, block, 1.0 /...  1.24 us
    pallas_call x1, Pallas kernels, local(): pl.pallas_call(functools.partial(lag_kernel, halves), out_shape=jax.Shape...  1.03 us
    pallas_call x1, Pallas kernels, local(): pl.pallas_call(functools.partial(bin_kernel, owners, bands, block, halves...  1.02 us

profile of v2, /device:TPU:0, one launch (start us, length us, event | category | flops | bytes accessed | tf_op | source)
XLA Modules:
  0.0 28.7 jit_solution(13314495559405555165)
XLA Ops:
  0.0 1.2 %shard_map.46 = (bf16[16,20,2,128]{3,2,1,0:T(2,128)(2,1)S(1)}, f32[1,1024]{1,0:T(1,128)S(1)}, bf16[256,192]{1,0:T(8,128)(2,1)S(1)}, f32[256,256]{1,0:T(8,128)S(1)}, bf16[16,512]{1,0:T(8,128)(2,1)S(1)}) custom-call(bf16[8,2,4096]{2,1,0:T(2,128)(2,1)} %spectra_ref.1, s32[1,256]{1,0:T(1,128)} %bitcast.4, s32[1,256]{1,0:T(1,128)} %bitcast.5, f32[1,1024]{1,0:T(1,128)} %stack_ref.1), custom_call_target="tpu_custom_call" | custom-call | tf_op jit(solution)/shard_map/pallas_call | solution.py:201
  1.2 15.6 %all_to_all.10.got_ref = bf16[16,40,128]{2,1,0:T(8,128)(2,1)S(1)} all-to-all(bf16[16,40,128]{2,1,0:T(8,128)(2,1)S(1)} %bitcast.3), channel_id=1, replica_groups=mesh['stn'=16,'frq'=2] {'stn'}, dimensions={0} | all-to-all | bytes 327680 | tf_op jit(solution)/shard_map/all_to_all | solution.py:218
  16.9 1.0 %shard_map.47 = f32[32,4,128]{2,1,0:T(4,128)S(1)} custom-call(bf16[16,40,128]{2,1,0:T(8,128)(2,1)S(1)} %all_to_all.10.got_ref), custom_call_target="tpu_custom_call" | custom-call | tf_op jit(solution)/shard_map/pallas_call | solution.py:219
  17.9 9.8 %all_to_all.11.sums_ref = f32[32,4,128]{2,1,0:T(4,128)S(1)} all-to-all(f32[32,4,128]{2,1,0:T(4,128)S(1)} %shard_map.47), channel_id=1, replica_groups=mesh['stn'=16,'frq'=2] {'stn','frq'}, dimensions={0} | all-to-all | bytes 131072 | tf_op jit(solution)/shard_map/all_to_all | solution.py:226
  27.7 1.0 %shard_map.48 = f32[1,1024]{1,0:T(1,128)} custom-call(bf16[256,192]{1,0:T(8,128)(2,1)S(1)} %get-tuple-element.10.first_ref, f32[256,256]{1,0:T(8,128)S(1)} %get-tuple-element.11.turn_ref, bf16[16,512]{1,0:T(8,128)(2,1)S(1)} %get-tuple-element.12.last_ref, f32[32,4,128]{2,1,0:T(4,128)S(1)} %all_to_all.11.sums_ref, f32[1,1024]{1,0:T(1,128)S(1)} %get-tuple-element.14.stack_ref), custom_call_target="tpu_custom_call" | custom-call | tf_op jit(solution)/shard_map/pallas_call | solution.py:227

commit v3 on v2

--- a/solution.py
+++ b/solution.py
@@ -24,11 +24,20 @@
     return upper, (value - upper.astype(jnp.float32)).astype(jnp.bfloat16)
 
 
+def listed(place, values):
+    found = jnp.zeros_like(place)
+    for index, value in enumerate(values):
+        found = jnp.where(place == index, value, found)
+    return found
+
+
 def dot(left, right):
     return jnp.dot(left, right, preferred_element_type=jnp.float32)
 
 
-def pack_kernel(owners, bands, block, scale, spectra_ref, bin_ref, valid_ref, stack_ref, *refs):
+def pack_kernel(
+    owners, block, scale, order, last_order, spectra_ref, bin_ref, valid_ref, stack_ref, *refs
+):
     pack_ref, held_ref, *tables, bins, valids, sems = refs
     stations = owners * block
     pairs = bins.shape[1]
@@ -42,12 +51,14 @@
     if len(spectra_ref.shape) == 3:
         halves = tiles // block
         for place in range(owners * halves):
-            source = spectra_ref.at[:, :, pl.ds(place * lanes, lanes)]
-            target = pack_ref.at[place // halves, pl.ds(place % halves * block, block)]
+            slot, half = place // halves, place % halves
+            source = spectra_ref.at[:, :, pl.ds((order[slot] * halves + half) * lanes, lanes)]
+            target = pack_ref.at[slot, pl.ds(half * block, block)]
             copies.append(pltpu.make_async_copy(source, target, sems.at[3 + place]))
     else:
-        target = pack_ref.at[:, pl.ds(0, tiles)]
-        copies.append(pltpu.make_async_copy(spectra_ref, target, sems.at[3]))
+        for slot in range(owners):
+            target = pack_ref.at[slot, pl.ds(0, tiles)]
+            copies.append(pltpu.make_async_copy(spectra_ref.at[order[slot]], target, sems.at[3 + slot]))
     for copy in copies:
         copy.start()
     place = iota((block, pairs), 1)
@@ -55,8 +66,10 @@
     place = iota((pairs, stations), 0)
     ahead = lax.axis_index("stn") + (owners - 1)
     other = lax.rem(ahead - lax.div(place, block * block), owners) * block + lax.rem(place, block)
-    right = jnp.where(other == iota((pairs, stations), 1), 1.0, 0.0).astype(jnp.bfloat16)
-    fill_tables(owners, bands, scale, *tables)
+    column = iota((1, stations), 1)
+    column = listed(lax.div(column, block), order) * block + lax.rem(column, block)
+    right = jnp.where(other == column, 1.0, 0.0).astype(jnp.bfloat16)
+    fill_tables(last_order, scale, *tables)
     copies[0].wait()
     copies[1].wait()
     codes = jnp.where(valids[...] != 0, bins[...] + 1, 0).astype(jnp.float32)
@@ -72,7 +85,7 @@
         copy.wait()
 
 
-def bin_kernel(owners, copies, block, halves, got_ref, sums_ref, rows_ref):
+def bin_kernel(owners, block, halves, last_order, got_ref, sums_ref, rows_ref):
     stations = owners * block
     lanes = got_ref.shape[2]
     start = 2 * halves * block
@@ -103,8 +116,9 @@
             mix_im = mixed[:, (2 * half + 1) * lanes : (2 * half + 2) * lanes]
             real = jnp.sum(own_re * mix_re + own_im * mix_im, axis=0, keepdims=True)
             imag = jnp.sum(own_im * mix_re - own_re * mix_im, axis=0, keepdims=True)
-            for copy in range(copies):
-                place = owner * copies + copy
+            for place in range(len(last_order)):
+                if last_order[place] % owners != owner:
+                    continue
                 sums_ref[place, half : half + 1, :] = real
                 sums_ref[place, halves + half : halves + half + 1, :] = imag
 
@@ -123,15 +137,14 @@
         store(step * TILE, near_cos * cos - near_sin * sin, near_sin * cos + near_cos * sin)
 
 
-def fill_tables(owners, bands, scale, first_ref, turn_ref, last_ref):
+def fill_tables(last_order, scale, first_ref, turn_ref, last_ref):
     coarse, span = first_ref.shape[0] // 2, first_ref.shape[1] // 3
     turns, fine = last_ref.shape[0] // 2, last_ref.shape[1] // 2
 
-    width = max(span, LANES)
+    width, sources = max(span, LANES), len(last_order)
     column = lax.rem(iota((1, width), 1), span)
-    source = lax.rem(column, owners * bands)
-    factor = lax.rem(source, bands) * owners + lax.div(source, bands)
-    ahead = jnp.where(column < owners * bands, 0.0, 0.5 * math.pi)
+    factor = listed(lax.rem(column, sources), last_order)
+    ahead = jnp.where(column < sources, 0.0, 0.5 * math.pi)
 
     def store_first(start, cos, sin):
         for begin, value in ((start, cos), (coarse + start, sin)):
@@ -148,6 +161,7 @@
     powers(iota((1, fine), 1) + 1, SAMPLES, coarse, store_turn)
     shape = (turns, fine)
     band = lax.axis_index("frq")
+    bands = lax.axis_size("frq")
     step = iota(shape, 0) + band * turns + (SAMPLES - bands * turns // 2)
     cos, sin = turn((iota(shape, 1) + 1) * step, fine)
     upper, lower = split(jnp.concatenate([cos, -sin], axis=1) * scale)
@@ -176,6 +190,14 @@
         out_ref[:, place] = stack_ref[:, place] + lags[row : row + 1, :]
 
 
+def orders(owners, bands):
+    part = owners // 4
+    within = range(part - 1, -1, -1)
+    order = [outer * part + inner for outer in (1, 0, 2, 3) for inner in within]
+    last = [(band, outer) for outer in range(4) for band in range(bands)]
+    return order, [band * owners + outer * part + inner for band, outer in last for inner in within]
+
+
 def whole(memory=pltpu.VMEM):
     return pl.BlockSpec(memory_space=memory)
 
@@ -194,12 +216,13 @@
     halves = fine // lanes
     coarse = SAMPLES // fine
     turns = stack_in.shape[1] // coarse
+    order, last_order = orders(owners, bands)
     if lanes < LANES:
         spectra = spectra.reshape(block, 2, owners, halves, lanes).transpose(2, 3, 0, 1, 4)
         spectra = spectra.reshape(owners, halves * block, 2, lanes)
     rows = halves * block + stations // lanes * (block // 2)
     packed, stack, *tables = pl.pallas_call(
-        functools.partial(pack_kernel, owners, bands, block, 1.0 / (width * bands)),
+        functools.partial(pack_kernel, owners, block, 1.0 / (width * bands), order, last_order),
         out_shape=[
             pltpu.VMEM((owners, rows, 2, lanes), jnp.bfloat16),
             pltpu.VMEM(stack_in.shape, jnp.float32),
@@ -215,15 +238,17 @@
             pltpu.SemaphoreType.DMA((3 + owners * halves,)),
         ],
     )(spectra, pair_bin.reshape(1, pairs), pair_valid.reshape(1, pairs), stack_in)
-    got = lax.all_to_all(packed.reshape(owners, 2 * rows, lanes), "stn", 0, 0, tiled=True)
+    packed = packed.reshape(owners, 2 * rows, lanes)
+    got = lax.all_to_all(packed, "stn", 0, 0, axis_index_groups=[order], tiled=True)
     sums = pl.pallas_call(
-        functools.partial(bin_kernel, owners, bands, block, halves),
+        functools.partial(bin_kernel, owners, block, halves, last_order),
         out_shape=pltpu.VMEM((owners * bands, 2 * halves, lanes), jnp.float32),
         in_specs=[whole()],
         out_specs=whole(),
         scratch_shapes=[pltpu.VMEM((halves, 2 * stations, lanes), jnp.float32)],
     )(near(got))
-    sums = lax.all_to_all(sums, ("stn", "frq"), 0, 0, tiled=True)
+    axes = ("frq", "stn")
+    sums = lax.all_to_all(sums, axes, 0, 0, axis_index_groups=[last_order], tiled=True)
     return pl.pallas_call(
         functools.partial(lag_kernel, halves),
         out_shape=jax.ShapeDtypeStruct(stack_in.shape, jnp.float32),

time: 28.9 us -> 26.9 us (0.931)
  blocking collectives: 25.4 us -> 23.4 us
    all_to_all x2, blocking collectives: 25.4 us -> 23.4 us  [the longest x1 12.6 us: local(): lax.all_to_all(packed, 'stn', 0, 0, axis_index_groups=[order], tiled=True)]
where the time goes in v3:
time: 26.9 us; the launch traced here: 26.7 us
  blocking collectives  23.4 us (87%)
  Pallas kernels  3.28 us (12%)
    all_to_all x1, blocking collectives, local(): lax.all_to_all(packed, 'stn', 0, 0, axis_index_groups=[order], tiled=True)  12.6 us
    all_to_all x1, blocking collectives, local(): lax.all_to_all(sums, axes, 0, 0, axis_index_groups=[last_order], tiled=True)  10.7 us
    pallas_call x1, Pallas kernels, local(): pl.pallas_call(functools.partial(pack_kernel, owners, block, 1.0 / (width...  1.24 us
    pallas_call x1, Pallas kernels, local(): pl.pallas_call(functools.partial(lag_kernel, halves), out_shape=jax.Shape...  1.03 us
    pallas_call x1, Pallas kernels, local(): pl.pallas_call(functools.partial(bin_kernel, owners, block, halves, last_...  1.02 us

profile of v3, /device:TPU:0, one launch (start us, length us, event | category | flops | bytes accessed | tf_op | source)
XLA Modules:
  0.0 26.7 jit_solution(4145307886259037199)
XLA Ops:
  0.0 1.2 %shard_map.46 = (bf16[16,20,2,128]{3,2,1,0:T(2,128)(2,1)S(1)}, f32[1,1024]{1,0:T(1,128)S(1)}, bf16[256,192]{1,0:T(8,128)(2,1)S(1)}, f32[256,256]{1,0:T(8,128)S(1)}, bf16[16,512]{1,0:T(8,128)(2,1)S(1)}) custom-call(bf16[8,2,4096]{2,1,0:T(2,128)(2,1)} %spectra_ref.1, s32[1,256]{1,0:T(1,128)} %bitcast.4, s32[1,256]{1,0:T(1,128)} %bitcast.5, f32[1,1024]{1,0:T(1,128)} %stack_ref.1), custom_call_target="tpu_custom_call" | custom-call | tf_op jit(solution)/shard_map/pallas_call | solution.py:224
  1.2 12.6 %all_to_all.10.got_ref = bf16[16,40,128]{2,1,0:T(8,128)(2,1)S(1)} all-to-all(bf16[16,40,128]{2,1,0:T(8,128)(2,1)S(1)} %bitcast.3), channel_id=1, replica_groups={{14,12,10,8,6,4,2,0,22,20,18,16,30,28,26,24},{15,13,11,9,7,5,3,1,23,21,..., dimensions={0} | all-to-all | bytes 327680 | tf_op jit(solution)/shard_map/all_to_all | solution.py:242
  13.9 1.0 %shard_map.47 = f32[32,4,128]{2,1,0:T(4,128)S(1)} custom-call(bf16[16,40,128]{2,1,0:T(8,128)(2,1)S(1)} %all_to_all.10.got_ref), custom_call_target="tpu_custom_call" | custom-call | tf_op jit(solution)/shard_map/pallas_call | solution.py:243
  14.9 10.7 %all_to_all.11.sums_ref = f32[32,4,128]{2,1,0:T(4,128)S(1)} all-to-all(f32[32,4,128]{2,1,0:T(4,128)S(1)} %shard_map.47), channel_id=1, replica_groups={{6,4,2,0,7,5,3,1,14,12,10,8,15,13,11,9,22,20,18,16,23,21,19,17,30,28,26..., dimensions={0} | all-to-all | bytes 131072 | tf_op jit(solution)/shard_map/all_to_all | solution.py:251
  25.6 1.0 %shard_map.48 = f32[1,1024]{1,0:T(1,128)} custom-call(bf16[256,192]{1,0:T(8,128)(2,1)S(1)} %get-tuple-element.10.first_ref, f32[256,256]{1,0:T(8,128)S(1)} %get-tuple-element.11.turn_ref, bf16[16,512]{1,0:T(8,128)(2,1)S(1)} %get-tuple-element.12.last_ref, f32[32,4,128]{2,1,0:T(4,128)S(1)} %all_to_all.11.sums_ref, f32[1,1024]{1,0:T(1,128)S(1)} %get-tuple-element.14.stack_ref), custom_call_target="tpu_custom_call" | custom-call | tf_op jit(solution)/shard_map/pallas_call | solution.py:252

commit v4 on v3

--- a/solution.py
+++ b/solution.py
@@ -39,7 +39,6 @@
     owners, block, scale, order, last_order, spectra_ref, bin_ref, valid_ref, stack_ref, *refs
 ):
     pack_ref, held_ref, *tables, bins, valids, sems = refs
-    stations = owners * block
     pairs = bins.shape[1]
     lanes = pack_ref.shape[3]
     copies = [
@@ -47,7 +46,8 @@
         pltpu.make_async_copy(valid_ref, valids, sems.at[1]),
         pltpu.make_async_copy(stack_ref, held_ref, sems.at[2]),
     ]
-    tiles = pack_ref.shape[1] - stations // lanes * (block // 2)
+    rows = pairs // lanes
+    tiles = pack_ref.shape[1] - rows // 2
     if len(spectra_ref.shape) == 3:
         halves = tiles // block
         for place in range(owners * halves):
@@ -61,47 +61,76 @@
             copies.append(pltpu.make_async_copy(spectra_ref.at[order[slot]], target, sems.at[3 + slot]))
     for copy in copies:
         copy.start()
-    place = iota((block, pairs), 1)
-    mine = lax.rem(lax.div(place, block), block) == iota((block, pairs), 0)
-    place = iota((pairs, stations), 0)
+    reach = ROUNDS * block
+    place = iota((TILE, pairs), 1)
+    row = lax.div(lax.rem(lax.div(place, block), block), lanes // reach)
+    mine = row == iota((TILE, pairs), 0)
+    place = iota((pairs, lanes), 0)
     ahead = lax.axis_index("stn") + (owners - 1)
-    other = lax.rem(ahead - lax.div(place, block * block), owners) * block + lax.rem(place, block)
-    column = iota((1, stations), 1)
-    column = listed(lax.div(column, block), order) * block + lax.rem(column, block)
-    right = jnp.where(other == column, 1.0, 0.0).astype(jnp.bfloat16)
+    other = lax.rem(ahead - lax.div(place, block * block), owners)
+    station = lax.rem(lax.div(place, block), block)
+    column = lax.rem(station, lanes // reach) * reach + lax.rem(other, ROUNDS) * block
+    right = column + lax.rem(place, block) == iota((pairs, lanes), 1)
+    right = jnp.where(right, 1.0, 0.0).astype(jnp.bfloat16)
     fill_tables(last_order, scale, *tables)
     copies[0].wait()
     copies[1].wait()
     codes = jnp.where(valids[...] != 0, bins[...] + 1, 0).astype(jnp.float32)
-    left = jnp.where(mine, jnp.broadcast_to(codes, (block, pairs)), 0.0).astype(jnp.bfloat16)
-    codes = dot(left, right)
-    for place in range(stations // lanes):
-        piece = codes[:, place * lanes : (place + 1) * lanes].reshape(block // 2, 2, lanes)
-        piece = piece.astype(jnp.bfloat16)
-        start = tiles + place * (block // 2)
-        for owner in range(owners):
-            pack_ref[owner, start : start + block // 2] = piece
+    left = jnp.where(mine, jnp.broadcast_to(codes, (TILE, pairs)), 0.0).astype(jnp.bfloat16)
+    codes = dot(left, right)[:rows].reshape(rows // 2, 2, lanes).astype(jnp.bfloat16)
+    for slot in range(owners):
+        pack_ref[slot, tiles:] = codes
     for copy in copies[2:]:
         copy.wait()
 
 
-def bin_kernel(owners, block, halves, last_order, got_ref, sums_ref, rows_ref):
-    stations = owners * block
-    lanes = got_ref.shape[2]
-    start = 2 * halves * block
-    codes = [
-        got_ref[:, start + place * block : start + (place + 1) * block, :].reshape(stations, lanes)
-        for place in range(stations // lanes)
-    ]
-    codes = jnp.concatenate(codes, axis=1).astype(jnp.float32)
+def code_grid(order, block, slab, start, rows_ref):
+    owners, lanes = len(order), rows_ref.shape[1]
+    stations, reach = owners * block, ROUNDS * block
+    shape = (block, lanes)
+    span = lanes // reach
+    row, place = iota(shape, 0), iota(shape, 1)
+    seen = lax.rem(row, span) == lax.div(place, reach)
+    seen = [seen & (lax.div(row, span) == part) for part in range(block // span)]
+    lines = []
+    for slot in range(owners):
+        line = jnp.zeros(shape, jnp.float32)
+        for part, chosen in enumerate(seen):
+            place = slot * slab + start + part
+            line = jnp.where(chosen, jnp.broadcast_to(rows_ref[place : place + 1, :], shape), line)
+        lines.append(line)
+    lines = jnp.concatenate(lines, axis=0).astype(jnp.bfloat16)
+    shape = (lanes, stations)
+    device = listed(lax.div(iota((1, stations), 1), block), order)
+    column = lax.rem(device, ROUNDS) * block + lax.rem(iota((1, stations), 1), block)
+    spread = jnp.where(lax.rem(iota(shape, 0), reach) == column, 1.0, 0.0).astype(jnp.bfloat16)
+    codes = dot(lines, spread)
+    device = jnp.broadcast_to(device, (block, stations))
+    lines = []
+    for slot in range(owners):
+        apart = order[slot] - 1 - device
+        paired = ((apart >= 0) & (apart < ROUNDS)) | (apart < ROUNDS - owners)
+        lines.append(jnp.where(paired, codes[slot * block : (slot + 1) * block], 0.0))
+    return jnp.concatenate(lines, axis=0)
+
+
+def bin_kernel(block, halves, order, last_order, got_ref, sums_ref, rows_ref):
+    owners, lanes = len(order), got_ref.shape[1]
+    slab, start = got_ref.shape[0] // owners, 2 * halves * block
+    rows_ref[...] = got_ref[...].astype(jnp.float32)
+    codes = code_grid(order, block, slab, start, rows_ref)
     shape = (lanes, lanes)
     same = lax.div(iota(shape, 0), WBLK) == lax.div(iota(shape, 1), WBLK)
     same = jnp.where(same, 0.5 / WBLK, 0.0).astype(jnp.bfloat16)
     pieces = []
     for half in range(halves):
-        raw = got_ref[:, 2 * half * block : 2 * (half + 1) * block, :].astype(jnp.float32)
-        rows_ref[half] = raw.reshape(2 * stations, lanes)
-        raw = [rows_ref[half, pl.ds(part, stations, stride=2), :] for part in range(2)]
+        raw = []
+        for part in range(2):
+            first = 2 * half * block + part
+            lines = [
+                rows_ref[pl.ds(slot * slab + first, block, stride=2), :] for slot in range(owners)
+            ]
+            raw.append(jnp.concatenate(lines, axis=0))
         upper, lower = split(raw[0] * raw[0] + raw[1] * raw[1])
         scale = lax.rsqrt(dot(upper, same) + dot(lower, same) + 1e-06)
         pieces += [(value * scale).astype(jnp.bfloat16) for value in raw]
@@ -209,7 +238,6 @@
 def local(spectra, pair_bin, pair_valid, stack_in):
     block, _, width = spectra.shape
     owners, bands = lax.axis_size("stn"), lax.axis_size("frq")
-    stations = owners * block
     pairs = pair_valid.shape[0]
     fine = width // owners
     lanes = min(fine, LANES)
@@ -220,11 +248,11 @@
     if lanes < LANES:
         spectra = spectra.reshape(block, 2, owners, halves, lanes).transpose(2, 3, 0, 1, 4)
         spectra = spectra.reshape(owners, halves * block, 2, lanes)
-    rows = halves * block + stations // lanes * (block // 2)
+    slab = 2 * halves * block + pairs // lanes
     packed, stack, *tables = pl.pallas_call(
         functools.partial(pack_kernel, owners, block, 1.0 / (width * bands), order, last_order),
         out_shape=[
-            pltpu.VMEM((owners, rows, 2, lanes), jnp.bfloat16),
+            pltpu.VMEM((owners, slab // 2, 2, lanes), jnp.bfloat16),
             pltpu.VMEM(stack_in.shape, jnp.float32),
             pltpu.VMEM((2 * coarse, 6 * owners * bands), jnp.bfloat16),
             pltpu.VMEM((2 * coarse, fine), jnp.float32),
@@ -238,14 +266,14 @@
             pltpu.SemaphoreType.DMA((3 + owners * halves,)),
         ],
     )(spectra, pair_bin.reshape(1, pairs), pair_valid.reshape(1, pairs), stack_in)
-    packed = packed.reshape(owners, 2 * rows, lanes)
     got = lax.all_to_all(packed, "stn", 0, 0, axis_index_groups=[order], tiled=True)
+    got = got.reshape(owners * slab, lanes)
     sums = pl.pallas_call(
-        functools.partial(bin_kernel, owners, block, halves, last_order),
+        functools.partial(bin_kernel, block, halves, order, last_order),
         out_shape=pltpu.VMEM((owners * bands, 2 * halves, lanes), jnp.float32),
         in_specs=[whole()],
         out_specs=whole(),
-        scratch_shapes=[pltpu.VMEM((halves, 2 * stations, lanes), jnp.float32)],
+        scratch_shapes=[pltpu.VMEM((owners * slab, lanes), jnp.float32)],
     )(near(got))
     axes = ("frq", "stn")
     sums = lax.all_to_all(sums, axes, 0, 0, axis_index_groups=[last_order], tiled=True)

time: 26.9 us -> 26.4 us (0.981)
  blocking collectives: 23.4 us -> 22.9 us
    all_to_all x1, blocking collectives: 12.6 us -> 12.2 us  [local(): lax.all_to_all(packed, 'stn', 0, 0, axis_index_groups=[order], tiled=True)]
where the time goes in v4:
time: 26.4 us; the launch traced here: 26.2 us
  blocking collectives  22.9 us (87%)
  Pallas kernels  3.23 us (12%)
    all_to_all x1, blocking collectives, local(): lax.all_to_all(packed, 'stn', 0, 0, axis_index_groups=[order], tiled=True)  12.2 us
    all_to_all x1, blocking collectives, local(): lax.all_to_all(sums, axes, 0, 0, axis_index_groups=[last_order], tiled=True)  10.7 us
    pallas_call x1, Pallas kernels, local(): pl.pallas_call(functools.partial(pack_kernel, owners, block, 1.0 / (width...  1.24 us
    pallas_call x1, Pallas kernels, local(): pl.pallas_call(functools.partial(lag_kernel, halves), out_shape=jax.Shape...  1.03 us
    pallas_call x1, Pallas kernels, local(): pl.pallas_call(functools.partial(bin_kernel, block, halves, order, last_o...  0.97 us

profile of v4, /device:TPU:0, one launch (start us, length us, event | category | flops | bytes accessed | tf_op | source)
XLA Modules:
  0.0 26.2 jit_solution(5420977085599046740)
XLA Ops:
  0.0 1.2 %shard_map.46 = (bf16[16,17,2,128]{3,2,1,0:T(2,128)(2,1)S(1)}, f32[1,1024]{1,0:T(1,128)S(1)}, bf16[256,192]{1,0:T(8,128)(2,1)S(1)}, f32[256,256]{1,0:T(8,128)S(1)}, bf16[16,512]{1,0:T(8,128)(2,1)S(1)}) custom-call(bf16[8,2,4096]{2,1,0:T(2,128)(2,1)} %spectra_ref.1, s32[1,256]{1,0:T(1,128)} %bitcast.4, s32[1,256]{1,0:T(1,128)} %bitcast.5, f32[1,1024]{1,0:T(1,128)} %stack_ref.1), custom_call_target="tpu_custom_call" | custom-call | tf_op jit(solution)/shard_map/pallas_call | solution.py:252
  1.2 12.2 %all_to_all.10 = bf16[16,17,2,128]{3,2,1,0:T(2,128)(2,1)S(1)} all-to-all(bf16[16,17,2,128]{3,2,1,0:T(2,128)(2,1)S(1)} %get-tuple-element.13), channel_id=1, replica_groups={{14,12,10,8,6,4,2,0,22,20,18,16,30,28,26,24},{15,13,11,9,7,5,3,1,23,21,..., dimensions={0} | all-to-all | bytes 278528 | tf_op jit(solution)/shard_map/all_to_all | solution.py:269
  13.5 1.0 %shard_map.47 = f32[32,4,128]{2,1,0:T(4,128)S(1)} custom-call(bf16[544,128]{1,0:T(8,128)(2,1)S(1)} %bitcast.3), custom_call_target="tpu_custom_call" | custom-call | tf_op jit(solution)/shard_map/pallas_call | solution.py:271
  14.5 10.7 %all_to_all.11.sums_ref = f32[32,4,128]{2,1,0:T(4,128)S(1)} all-to-all(f32[32,4,128]{2,1,0:T(4,128)S(1)} %shard_map.47), channel_id=1, replica_groups={{6,4,2,0,7,5,3,1,14,12,10,8,15,13,11,9,22,20,18,16,23,21,19,17,30,28,26..., dimensions={0} | all-to-all | bytes 131072 | tf_op jit(solution)/shard_map/all_to_all | solution.py:279
  25.1 1.0 %shard_map.48 = f32[1,1024]{1,0:T(1,128)} custom-call(bf16[256,192]{1,0:T(8,128)(2,1)S(1)} %get-tuple-element.10.first_ref, f32[256,256]{1,0:T(8,128)S(1)} %get-tuple-element.11.turn_ref, bf16[16,512]{1,0:T(8,128)(2,1)S(1)} %get-tuple-element.12.last_ref, f32[32,4,128]{2,1,0:T(4,128)S(1)} %all_to_all.11.sums_ref, f32[1,1024]{1,0:T(1,128)S(1)} %get-tuple-element.14.stack_ref), custom_call_target="tpu_custom_call" | custom-call | tf_op jit(solution)/shard_map/pallas_call | solution.py:280

commit v5 on v4

--- a/solution.py
+++ b/solution.py
@@ -118,7 +118,8 @@
     owners, lanes = len(order), got_ref.shape[1]
     slab, start = got_ref.shape[0] // owners, 2 * halves * block
     rows_ref[...] = got_ref[...].astype(jnp.float32)
-    codes = code_grid(order, block, slab, start, rows_ref)
+    codes = code_grid(order, block, slab, start, rows_ref).astype(jnp.bfloat16)
+    one, zero = jnp.ones((), jnp.bfloat16), jnp.zeros((), jnp.bfloat16)
     shape = (lanes, lanes)
     same = lax.div(iota(shape, 0), WBLK) == lax.div(iota(shape, 1), WBLK)
     same = jnp.where(same, 0.5 / WBLK, 0.0).astype(jnp.bfloat16)
@@ -137,7 +138,7 @@
     right = jnp.concatenate(pieces, axis=1)
     left = [piece.astype(jnp.float32) for piece in pieces]
     for owner in range(owners):
-        chosen = jnp.where(codes == float(owner + 1), 1.0, 0.0).astype(jnp.bfloat16)
+        chosen = jnp.where(codes == jnp.bfloat16(owner + 1), one, zero)
         mixed = dot(chosen, right)
         for half in range(halves):
             own_re, own_im = left[2 * half], left[2 * half + 1]
@@ -222,7 +223,7 @@
 def orders(owners, bands):
     part = owners // 4
     within = range(part - 1, -1, -1)
-    order = [outer * part + inner for outer in (1, 0, 2, 3) for inner in within]
+    order = [outer * part + inner for outer in (2, 3, 1, 0) for inner in within]
     last = [(band, outer) for outer in range(4) for band in range(bands)]
     return order, [band * owners + outer * part + inner for band, outer in last for inner in within]
 

time: 26.4 us -> 26.3 us (level)
    all_to_all x1, blocking collectives: 12.2 us -> 11.3 us  [local(): lax.all_to_all(packed, 'stn', 0, 0, axis_index_groups=[order], tiled=True)]
    all_to_all x1, blocking collectives: 10.7 us -> 11.6 us  [local(): lax.all_to_all(sums, axes, 0, 0, axis_index_groups=[last_order], tiled=True)]
where the time goes in v5:
time: 26.3 us; the launch traced here: 26.1 us
  blocking collectives  22.9 us (87%)
  Pallas kernels  3.22 us (12%)
    all_to_all x1, blocking collectives, local(): lax.all_to_all(sums, axes, 0, 0, axis_index_groups=[last_order], tiled=True)  11.6 us
    all_to_all x1, blocking collectives, local(): lax.all_to_all(packed, 'stn', 0, 0, axis_index_groups=[order], tiled=True)  11.3 us
    pallas_call x1, Pallas kernels, local(): pl.pallas_call(functools.partial(pack_kernel, owners, block, 1.0 / (width...  1.24 us
    pallas_call x1, Pallas kernels, local(): pl.pallas_call(functools.partial(lag_kernel, halves), out_shape=jax.Shape...  1.03 us
    pallas_call x1, Pallas kernels, local(): pl.pallas_call(functools.partial(bin_kernel, block, halves, order, last_o...  0.95 us

profile of v5, /device:TPU:0, one launch (start us, length us, event | category | flops | bytes accessed | tf_op | source)
XLA Modules:
  0.0 26.1 jit_solution(9023507276136574947)
XLA Ops:
  0.0 1.2 %shard_map.46 = (bf16[16,17,2,128]{3,2,1,0:T(2,128)(2,1)S(1)}, f32[1,1024]{1,0:T(1,128)S(1)}, bf16[256,192]{1,0:T(8,128)(2,1)S(1)}, f32[256,256]{1,0:T(8,128)S(1)}, bf16[16,512]{1,0:T(8,128)(2,1)S(1)}) custom-call(bf16[8,2,4096]{2,1,0:T(2,128)(2,1)} %spectra_ref.1, s32[1,256]{1,0:T(1,128)} %bitcast.4, s32[1,256]{1,0:T(1,128)} %bitcast.5, f32[1,1024]{1,0:T(1,128)} %stack_ref.1), custom_call_target="tpu_custom_call" | custom-call | tf_op jit(solution)/shard_map/pallas_call | solution.py:253
  1.2 11.3 %all_to_all.10 = bf16[16,17,2,128]{3,2,1,0:T(2,128)(2,1)S(1)} all-to-all(bf16[16,17,2,128]{3,2,1,0:T(2,128)(2,1)S(1)} %get-tuple-element.13), channel_id=1, replica_groups={{22,20,18,16,30,28,26,24,14,12,10,8,6,4,2,0},{23,21,19,17,31,29,27,25,1..., dimensions={0} | all-to-all | bytes 278528 | tf_op jit(solution)/shard_map/all_to_all | solution.py:270
  12.6 0.9 %shard_map.47 = f32[32,4,128]{2,1,0:T(4,128)S(1)} custom-call(bf16[544,128]{1,0:T(8,128)(2,1)S(1)} %bitcast.3), custom_call_target="tpu_custom_call" | custom-call | tf_op jit(solution)/shard_map/pallas_call | solution.py:272
  13.5 11.6 %all_to_all.11.sums_ref = f32[32,4,128]{2,1,0:T(4,128)S(1)} all-to-all(f32[32,4,128]{2,1,0:T(4,128)S(1)} %shard_map.47), channel_id=1, replica_groups={{6,4,2,0,7,5,3,1,14,12,10,8,15,13,11,9,22,20,18,16,23,21,19,17,30,28,26..., dimensions={0} | all-to-all | bytes 131072 | tf_op jit(solution)/shard_map/all_to_all | solution.py:280
  25.1 1.0 %shard_map.48 = f32[1,1024]{1,0:T(1,128)} custom-call(bf16[256,192]{1,0:T(8,128)(2,1)S(1)} %get-tuple-element.10.first_ref, f32[256,256]{1,0:T(8,128)S(1)} %get-tuple-element.11.turn_ref, bf16[16,512]{1,0:T(8,128)(2,1)S(1)} %get-tuple-element.12.last_ref, f32[32,4,128]{2,1,0:T(4,128)S(1)} %all_to_all.11.sums_ref, f32[1,1024]{1,0:T(1,128)S(1)} %get-tuple-element.14.stack_ref), custom_call_target="tpu_custom_call" | custom-call | tf_op jit(solution)/shard_map/pallas_call | solution.py:281

commit v6 on v4

--- a/solution.py
+++ b/solution.py
@@ -148,8 +148,8 @@
             for place in range(len(last_order)):
                 if last_order[place] % owners != owner:
                     continue
-                sums_ref[place, half : half + 1, :] = real
-                sums_ref[place, halves + half : halves + half + 1, :] = imag
+                sums_ref[place, half : half + 1, :] = real.astype(sums_ref.dtype)
+                sums_ref[place, halves + half : halves + half + 1, :] = imag.astype(sums_ref.dtype)
 
 
 def turn(product, period, ahead=0.0):
@@ -200,7 +200,7 @@
 def lag_kernel(halves, first_ref, turn_ref, last_ref, sums_ref, stack_ref, out_ref):
     coarse = first_ref.shape[0] // 2
     turns = last_ref.shape[0] // 2
-    part = lambda row: sums_ref[:, row, :]
+    part = lambda row: sums_ref[:, row, :].astype(jnp.float32)
     real = jnp.concatenate([part(half) for half in range(halves)], axis=1)
     imag = jnp.concatenate([part(halves + half) for half in range(halves)], axis=1)
     upper, lower = split(jnp.concatenate([real, imag], axis=0))
@@ -270,7 +270,7 @@
     got = got.reshape(owners * slab, lanes)
     sums = pl.pallas_call(
         functools.partial(bin_kernel, block, halves, order, last_order),
-        out_shape=pltpu.VMEM((owners * bands, 2 * halves, lanes), jnp.float32),
+        out_shape=pltpu.VMEM((owners * bands, 2 * halves, lanes), jnp.bfloat16),
         in_specs=[whole()],
         out_specs=whole(),
         scratch_shapes=[pltpu.VMEM((owners * slab, lanes), jnp.float32)],

time: 26.4 us -> 26.4 us (level)
  no operation moved by 1% of the time
where the time goes in v6:
time: 26.4 us; the launch traced here: 26.2 us
  blocking collectives  22.9 us (87%)
  Pallas kernels  3.29 us (12%)
    all_to_all x1, blocking collectives, local(): lax.all_to_all(packed, 'stn', 0, 0, axis_index_groups=[order], tiled=True)  12.2 us
    all_to_all x1, blocking collectives, local(): lax.all_to_all(sums, axes, 0, 0, axis_index_groups=[last_order], tiled=True)  10.6 us
    pallas_call x1, Pallas kernels, local(): pl.pallas_call(functools.partial(pack_kernel, owners, block, 1.0 / (width...  1.24 us
    pallas_call x1, Pallas kernels, local(): pl.pallas_call(functools.partial(lag_kernel, halves), out_shape=jax.Shape...  1.05 us
    pallas_call x1, Pallas kernels, local(): pl.pallas_call(functools.partial(bin_kernel, block, halves, order, last_o...  1.01 us

profile of v6, /device:TPU:0, one launch (start us, length us, event | category | flops | bytes accessed | tf_op | source)
XLA Modules:
  0.0 26.2 jit_solution(2828014081231360575)
XLA Ops:
  0.0 1.2 %shard_map.46 = (bf16[16,17,2,128]{3,2,1,0:T(2,128)(2,1)S(1)}, f32[1,1024]{1,0:T(1,128)S(1)}, bf16[256,192]{1,0:T(8,128)(2,1)S(1)}, f32[256,256]{1,0:T(8,128)S(1)}, bf16[16,512]{1,0:T(8,128)(2,1)S(1)}) custom-call(bf16[8,2,4096]{2,1,0:T(2,128)(2,1)} %spectra_ref.1, s32[1,256]{1,0:T(1,128)} %bitcast.4, s32[1,256]{1,0:T(1,128)} %bitcast.5, f32[1,1024]{1,0:T(1,128)} %stack_ref.1), custom_call_target="tpu_custom_call" | custom-call | tf_op jit(solution)/shard_map/pallas_call | solution.py:252
  1.2 12.2 %all_to_all.10 = bf16[16,17,2,128]{3,2,1,0:T(2,128)(2,1)S(1)} all-to-all(bf16[16,17,2,128]{3,2,1,0:T(2,128)(2,1)S(1)} %get-tuple-element.13), channel_id=1, replica_groups={{14,12,10,8,6,4,2,0,22,20,18,16,30,28,26,24},{15,13,11,9,7,5,3,1,23,21,..., dimensions={0} | all-to-all | bytes 278528 | tf_op jit(solution)/shard_map/all_to_all | solution.py:269
  13.5 1.0 %shard_map.47 = bf16[32,4,128]{2,1,0:T(4,128)(2,1)S(1)} custom-call(bf16[544,128]{1,0:T(8,128)(2,1)S(1)} %bitcast.3), custom_call_target="tpu_custom_call" | custom-call | tf_op jit(solution)/shard_map/pallas_call | solution.py:271
  14.5 10.6 %all_to_all.11.sums_ref = bf16[32,4,128]{2,1,0:T(4,128)(2,1)S(1)} all-to-all(bf16[32,4,128]{2,1,0:T(4,128)(2,1)S(1)} %shard_map.47), channel_id=1, replica_groups={{6,4,2,0,7,5,3,1,14,12,10,8,15,13,11,9,22,20,18,16,23,21,19,17,30,28,26..., dimensions={0} | all-to-all | bytes 65536 | tf_op jit(solution)/shard_map/all_to_all | solution.py:279
  25.1 1.1 %shard_map.48 = f32[1,1024]{1,0:T(1,128)} custom-call(bf16[256,192]{1,0:T(8,128)(2,1)S(1)} %get-tuple-element.10.first_ref, f32[256,256]{1,0:T(8,128)S(1)} %get-tuple-element.11.turn_ref, bf16[16,512]{1,0:T(8,128)(2,1)S(1)} %get-tuple-element.12.last_ref, bf16[32,4,128]{2,1,0:T(4,128)(2,1)S(1)} %all_to_all.11.sums_ref, f32[1,1024]{1,0:T(1,128)S(1)} %get-tuple-element.14.stack_ref), custom_call_target="tpu_custom_call" | custom-call | tf_op jit(solution)/shard_map/pallas_call | solution.py:280
